TPU v7x, 512 devices: a whole 4x8x8 slice. The times are simulated.
512 devices in a mesh: ctx: 64 (over z_hi, y, core), tp: 8 (over x, z_lo).
Axes of the slice: x: 4, y: 8, z: 8 (z_hi: 4, z_lo: 2; z = z_hi * 2 + z_lo), core: 2. Of those that a mesh axis runs over, the one named last changes fastest.
Arguments:
- query_in: bfloat16 [1024, 16384], P('tp', 'ctx'), may hold values from -6 to 6
- key_in: bfloat16 [1024, 16384], P('tp', 'ctx'), may hold values from -6 to 6
- value_in: bfloat16 [1024, 16384], P('tp', 'ctx'), may hold values from -6 to 6
- short_kernel: float32 [3, 1024, 7], P(None, 'tp'), may hold values from -2 to 2
- basis_weight: float32 [64, 33], replicated, may hold values from -96 to 96
- basis_bias: float32 [64], replicated, may hold values from -3.140625 to 3.140625
- filter_proj: float32 [1024, 64], P('tp'), may hold values from -0.75 to 0.75
- decay_rate: float32 [1024], P('tp'), as said below
- skip_gain: float32 [1024], P('tp'), may hold values from -3 to 3
- grad_out: bfloat16 [1024, 16384], P('tp', 'ctx'), may hold values from -6 to 6
Outputs:
- mixed: bfloat16 [1024, 16384], P('tp', 'ctx')
- grad_query: bfloat16 [1024, 16384], P('tp', 'ctx')
- grad_key: bfloat16 [1024, 16384], P('tp', 'ctx')
- grad_value: bfloat16 [1024, 16384], P('tp', 'ctx')
- grad_proj: float32 [1024, 64], P('tp')
- grad_basis: float32 [64, 33], replicated
Inputs may be any that keep to these rules, and one draw needn't show every extreme that they name: decay_rate is positive in every channel.
All inputs are finite; a program needn't handle non-finite values.
Results may differ from a plain program's by a relative error of at most 0.0066.
Values may be sent and summed in bfloat16 or wider, within the bound.
No kernel may reach another device: no remote copies, remote signals or barrier semaphores. Data moves between devices by JAX's collectives and lax.ppermute only.
A program may use at most 64 MiB of HBM per device.

v0:
```python
import math
import jax
import jax.numpy as jnp
from jax import lax
from jax.sharding import PartitionSpec as P

PRECISE = lax.Precision.HIGHEST


def passed_along(value, axis, steps):
    count = lax.axis_size(axis)
    leading, last = (max(0, -steps), min(count, count - steps))
    return lax.ppermute(value, axis, [(source, source + steps) for source in range(leading, last)])


def features(offset_pos, num_pos, seq_total, num_freq):
    positions = offset_pos + jnp.arange(num_pos, dtype=jnp.int32)
    pieces = [positions.astype(jnp.float32) / seq_total]
    for harmonic in range(1, num_freq + 1):
        angles = (harmonic * positions % seq_total).astype(jnp.float32) * (
            2.0 * math.pi / seq_total
        )
        pieces.append(jnp.cos(angles))
        pieces.append(jnp.sin(angles))
    return jnp.stack(pieces)


def window(decay_rate, offset_pos, num_pos, seq_total):
    positions = (offset_pos + jnp.arange(num_pos, dtype=jnp.int32)).astype(jnp.float32)
    energy = jnp.expm1(-2.0 * decay_rate) / jnp.expm1(-2.0 * decay_rate / seq_total)
    return (
        jnp.exp(-(decay_rate[:, None] * positions[None, :]) / seq_total) / jnp.sqrt(energy)[:, None]
    )


def featurize_rim(signal, before, kernel):
    extended = jnp.concatenate([before, signal], axis=1).astype(jnp.float32)
    num_taps = kernel.shape[1]
    rim_len = num_taps - 1
    num_tok = signal.shape[1]
    result = kernel[:, 0:1] * extended[:, rim_len:]
    for offset in range(1, num_taps):
        result = (
            result
            + kernel[:, offset : offset + 1]
            * extended[:, rim_len - offset : rim_len - offset + num_tok]
        )
    return result


def featurize_back(signal, following, kernel):
    extended = jnp.concatenate([signal, following], axis=1).astype(jnp.float32)
    num_taps = kernel.shape[1]
    num_tok = signal.shape[1]
    result = kernel[:, 0:1] * extended[:, :num_tok]
    for offset in range(1, num_taps):
        result = result + kernel[:, offset : offset + 1] * extended[:, offset : offset + num_tok]
    return result


def tables(num_rows, num_cols, modulus):
    row_ids = jnp.arange(num_rows, dtype=jnp.int32)[:, None]
    col_ids = jnp.arange(num_cols, dtype=jnp.int32)[None, :]
    angles = (row_ids * col_ids % modulus).astype(jnp.float32) * (-2.0 * math.pi / modulus)
    return (jnp.cos(angles), jnp.sin(angles))


def spectrum(signal, outer, twiddle, inner):
    num_chan = signal.shape[0]
    folded = signal.reshape(num_chan, outer[0].shape[1], inner[0].shape[0])
    section_re = jnp.einsum("kt,nts->nks", outer[0], folded, precision=PRECISE)
    section_im = jnp.einsum("kt,nts->nks", outer[1], folded, precision=PRECISE)
    turned_re = section_re * twiddle[0] - section_im * twiddle[1]
    turned_im = section_re * twiddle[1] + section_im * twiddle[0]
    spec_re = jnp.einsum("nks,sj->nkj", turned_re, inner[0], precision=PRECISE) - jnp.einsum(
        "nks,sj->nkj", turned_im, inner[1], precision=PRECISE
    )
    spec_im = jnp.einsum("nks,sj->nkj", turned_re, inner[1], precision=PRECISE) + jnp.einsum(
        "nks,sj->nkj", turned_im, inner[0], precision=PRECISE
    )
    return (spec_re, spec_im)


def restore(spec_re, spec_im, outer, twiddle, inner):
    num_chan = spec_re.shape[0]
    padded_len = outer[0].shape[0] * inner[0].shape[0]
    back_re = jnp.einsum("nkj,sj->nks", spec_re, inner[0], precision=PRECISE) + jnp.einsum(
        "nkj,sj->nks", spec_im, inner[1], precision=PRECISE
    )
    back_im = jnp.einsum("nkj,sj->nks", spec_im, inner[0], precision=PRECISE) - jnp.einsum(
        "nkj,sj->nks", spec_re, inner[1], precision=PRECISE
    )
    turned_re = back_re * twiddle[0] + back_im * twiddle[1]
    turned_im = back_im * twiddle[0] - back_re * twiddle[1]
    result = jnp.einsum("kt,nks->nts", outer[0], turned_re, precision=PRECISE) + jnp.einsum(
        "kt,nks->nts", outer[1], turned_im, precision=PRECISE
    )
    return result.reshape(num_chan, -1) * (1.0 / padded_len)


def convolve_forward(carried_chan, filter_chan, own_skip, transform_tables):
    outer, twiddle, inner = transform_tables
    carried_wide = carried_chan.astype(jnp.float32)
    carried_re, carried_im = spectrum(carried_wide, outer, twiddle, inner)
    filter_re, filter_im = spectrum(filter_chan.astype(jnp.float32), outer, twiddle, inner)
    conv_chan = restore(
        filter_re * carried_re - filter_im * carried_im,
        filter_re * carried_im + filter_im * carried_re,
        outer,
        twiddle,
        inner,
    )
    long_chan = (conv_chan + own_skip[:, None] * carried_wide).astype(jnp.bfloat16)
    return (long_chan, (carried_re, carried_im, filter_re, filter_im))


def convolve_backward(grad_chan, spectra, own_skip, transform_tables):
    outer, twiddle, inner = transform_tables
    carried_re, carried_im, filter_re, filter_im = spectra
    grad_chan_wide = grad_chan.astype(jnp.float32)
    grad_re, grad_im = spectrum(grad_chan_wide, outer, twiddle, inner)
    carried_grad_chan = (
        restore(
            filter_re * grad_re + filter_im * grad_im,
            filter_re * grad_im - filter_im * grad_re,
            outer,
            twiddle,
            inner,
        )
        + own_skip[:, None] * grad_chan_wide
    ).astype(jnp.bfloat16)
    filter_grad_chan = restore(
        carried_re * grad_re + carried_im * grad_im,
        carried_re * grad_im - carried_im * grad_re,
        outer,
        twiddle,
        inner,
    ).astype(jnp.bfloat16)
    return (carried_grad_chan, filter_grad_chan)


def on_device(
    query_in,
    key_in,
    value_in,
    short_kernel,
    basis_weight,
    basis_bias,
    filter_proj,
    decay_rate,
    skip_gain,
    grad_out,
):
    ctx_size = lax.axis_size("ctx")
    ctx_rank = lax.axis_index("ctx")
    tp_size = lax.axis_size("tp")
    num_tok = query_in.shape[1]
    chan_local = query_in.shape[0]
    seq_total = num_tok * ctx_size
    all_channels = chan_local * tp_size
    num_freq = (basis_weight.shape[1] - 1) // 2
    feat_width = basis_weight.shape[0]
    rim_len = short_kernel.shape[2] - 1
    tok_start = ctx_rank * num_tok
    rim_edge = num_tok - rim_len
    per_dev = chan_local // ctx_size
    chan_start = ctx_rank * per_dev
    own_skip = lax.dynamic_slice_in_dim(skip_gain, chan_start, per_dev)
    proj_scale = 1.0 / math.sqrt(seq_total)
    basis_scale = math.sqrt(feat_width / (seq_total * all_channels))
    before = passed_along(
        (query_in[:, rim_edge:], key_in[:, rim_edge:], value_in[:, rim_edge:]), "ctx", 1
    )
    query_feat = featurize_rim(query_in, before[0], short_kernel[0])
    key_feat = featurize_rim(key_in, before[1], short_kernel[1])
    value_feat = featurize_rim(value_in, before[2], short_kernel[2])
    carried = (key_feat * value_feat).astype(jnp.bfloat16)
    grad_wide = grad_out.astype(jnp.float32)
    grad_long = (grad_wide * query_feat).astype(jnp.bfloat16)
    basis_rows = features(tok_start, num_tok, seq_total, num_freq)
    hidden_in = (
        jnp.dot(basis_weight, basis_rows, precision=PRECISE, preferred_element_type=jnp.float32)
        + basis_bias[:, None]
    )
    activation = jnp.sin(hidden_in)
    envelope = window(decay_rate, tok_start, num_tok, seq_total)
    filter_tok = (
        jnp.dot(filter_proj, activation, precision=PRECISE, preferred_element_type=jnp.float32)
        * envelope
    ).astype(jnp.bfloat16)
    inner_len = 2 * ctx_size
    transform_tables = (
        tables(num_tok, num_tok // 2, num_tok),
        tables(num_tok, inner_len, 2 * seq_total),
        tables(inner_len, inner_len, inner_len),
    )
    spread = (
        lax.all_to_all(carried, "ctx", split_axis=0, concat_axis=1, tiled=True),
        lax.all_to_all(filter_tok, "ctx", split_axis=0, concat_axis=1, tiled=True),
    )
    carried_chan = spread[0]
    filter_chan = spread[1]
    long_chan, spectra = convolve_forward(carried_chan, filter_chan, own_skip, transform_tables)
    long_tok = lax.all_to_all(long_chan, "ctx", split_axis=1, concat_axis=0, tiled=True)
    grad_chan = lax.all_to_all(grad_long, "ctx", split_axis=0, concat_axis=1, tiled=True)
    carried_grad_chan, filter_grad_chan = convolve_backward(
        grad_chan, spectra, own_skip, transform_tables
    )
    returned = (
        lax.all_to_all(carried_grad_chan, "ctx", split_axis=1, concat_axis=0, tiled=True),
        lax.all_to_all(filter_grad_chan, "ctx", split_axis=1, concat_axis=0, tiled=True),
    )
    carried_grad = returned[0]
    filter_grad_tok = returned[1]
    long_wide = long_tok.astype(jnp.float32)
    mixed = (query_feat * long_wide).astype(jnp.bfloat16)
    grad_query_feat = (grad_wide * long_wide).astype(jnp.bfloat16)
    grad_raw = filter_grad_tok.astype(jnp.float32) * envelope
    part_proj = jnp.dot(
        grad_raw, activation.T, precision=PRECISE, preferred_element_type=jnp.float32
    )
    grad_hidden = jnp.dot(
        filter_proj.T, grad_raw, precision=PRECISE, preferred_element_type=jnp.float32
    ) * jnp.cos(hidden_in)
    part_basis = jnp.dot(
        grad_hidden, basis_rows.T, precision=PRECISE, preferred_element_type=jnp.float32
    )
    grad_proj = lax.psum(part_proj, "ctx") * proj_scale
    grad_basis = lax.psum(part_basis, ("ctx", "tp")) * basis_scale
    carried_grad_wide = carried_grad.astype(jnp.float32)
    grad_key_feat = (carried_grad_wide * value_feat).astype(jnp.bfloat16)
    grad_value_feat = (carried_grad_wide * key_feat).astype(jnp.bfloat16)
    following = passed_along(
        (grad_query_feat[:, :rim_len], grad_key_feat[:, :rim_len], grad_value_feat[:, :rim_len]),
        "ctx",
        -1,
    )
    grad_query = featurize_back(grad_query_feat, following[0], short_kernel[0]).astype(jnp.bfloat16)
    grad_key = featurize_back(grad_key_feat, following[1], short_kernel[1]).astype(jnp.bfloat16)
    grad_value = featurize_back(grad_value_feat, following[2], short_kernel[2]).astype(jnp.bfloat16)
    return (mixed, grad_query, grad_key, grad_value, grad_proj, grad_basis)


def solution(mesh):
    return jax.shard_map(
        on_device,
        mesh=mesh,
        in_specs=(
            P("tp", "ctx"),
            P("tp", "ctx"),
            P("tp", "ctx"),
            P(None, "tp", None),
            P(),
            P(),
            P("tp", None),
            P("tp"),
            P("tp"),
            P("tp", "ctx"),
        ),
        out_specs=(
            P("tp", "ctx"),
            P("tp", "ctx"),
            P("tp", "ctx"),
            P("tp", "ctx"),
            P("tp", None),
            P(),
        ),
        check_vma=False,
    )
```

profile of v0, /device:TPU:1, one launch (start us, length us, event | category | flops | bytes accessed | tf_op | source)
XLA Modules:
  0.0 538.5 jit_solution(8369667688324918726)
XLA Ops:
  1.5 4.6 collective-permute-start
  10.4 15.5 %all-to-all-start = ((bf16[64,2,256]{2,1,0:T(2,128)(2,1)}), bf16[64,2,256]{2,1,0:T(2,128)(2,1)S(1)}, u32[]{:S(2)}, u32[]{:S(2)}) async-start(bf16[64,2,256]{2,1,0:T(2,128)(2,1)} %all_to_all.60), calls=%async_computation | async-start | bytes 131072 | tf_op jit(solution)/shard_map/all_to_all | solution.py:199
  26.0 3.5 collective-permute-start.2
  29.6 2.2 collective-permute-start.1
  35.7 2.4 all-to-all-done
  38.1 9.7 %all-to-all-start.3 = ((bf16[64,2,256]{2,1,0:T(2,128)(2,1)}), bf16[64,2,256]{2,1,0:T(2,128)(2,1)S(1)}, u32[]{:S(2)}, u32[]{:S(2)}) async-start(bf16[64,2,256]{2,1,0:T(2,128)(2,1)} %all_to_all.67), calls=%async_computation.3 | async-start | bytes 131072 | tf_op jit(solution)/shard_map/all_to_all | solution.py:205
  51.7 7.9 %all-to-all-done.3 = bf16[64,2,256]{2,1,0:T(2,128)(2,1)S(1)} async-done(((bf16[64,2,256]{2,1,0:T(2,128)(2,1)}), bf16[64,2,256]{2,1,0:T(2,128)(2,1)S(1)}, u32[]{:S(2)}, u32[]{:S(2)}) %all-to-all-start.3) | async-done | bytes 65568 | tf_op jit(solution)/shard_map/all_to_all | solution.py:205
  67.6 11.5 %fusion.19 = f32[2,128,128]{2,1,0:T(8,128)S(1)} fusion(f32[2,256,128]{1,2,0:T(8,128)S(1)} %convolution_subtract_fusion.1, f32[2,256,128]{1,2,0:T(8,128)S(1)} %convolution_add_fusion.1, f32[256,128]{0,1:T(8,128)S(1)} %copy.206, f32[256,128]{0,1:T(8,128)S(1)} %copy.204), kind=kOutput, calls=%fused_computation.45 | convolution fusion | flops 101318656 | bytes 917504 | tf_op jit(solution)/shard_map/kt,nks->nts/dot_general | solution.py:95
  80.9 4.8 all-to-all-start.4
  86.0 12.0 %all-to-all-done.4 = bf16[2,64,256]{2,0,1:T(2,128)(2,1)S(1)} async-done(((bf16[2,64,256]{2,0,1:T(2,128)(2,1)}), bf16[2,64,256]{2,0,1:T(2,128)(2,1)S(1)}, u32[]{:S(2)}, u32[]{:S(2)}) %all-to-all-start.4) | async-done | bytes 65568 | tf_op jit(solution)/shard_map/all_to_all | solution.py:210
  98.5 2.3 collective-permute-start.5
  101.9 6.0 %all-to-all-start.1 = ((bf16[64,2,256]{2,1,0:T(2,128)(2,1)}), bf16[64,2,256]{2,1,0:T(2,128)(2,1)S(1)}, u32[]{:S(2)}, u32[]{:S(2)}) async-start(bf16[64,2,256]{2,1,0:T(2,128)(2,1)} %all_to_all.63), calls=%async_computation.1 | async-start | bytes 131072 | tf_op jit(solution)/shard_map/all_to_all | solution.py:198
  108.0 2.4 collective-permute-start.4
  110.4 1.0 fusion.37
  111.4 2.1 collective-permute-done.4
  113.5 1.0 fusion.44
  114.5 5.6 %all-to-all-done.1 = bf16[64,2,256]{2,1,0:T(2,128)(2,1)S(1)} async-done(((bf16[64,2,256]{2,1,0:T(2,128)(2,1)}), bf16[64,2,256]{2,1,0:T(2,128)(2,1)S(1)}, u32[]{:S(2)}, u32[]{:S(2)}) %all-to-all-start.1) | async-done | bytes 65568 | tf_op jit(solution)/shard_map/all_to_all | solution.py:198
  130.0 7.0 %all-to-all-start.5 = ((bf16[2,64,256]{2,0,1:T(2,128)(2,1)}), bf16[2,64,256]{2,0,1:T(2,128)(2,1)S(1)}, u32[]{:S(2)}, u32[]{:S(2)}) async-start(bf16[2,64,256]{2,0,1:T(2,128)(2,1)} %copy.242), calls=%async_computation.5 | async-start | bytes 131072 | tf_op jit(solution)/shard_map/all_to_all | solution.py:211
  142.3 6.9 %all-to-all-done.5 = bf16[2,64,256]{2,0,1:T(2,128)(2,1)S(1)} async-done(((bf16[2,64,256]{2,0,1:T(2,128)(2,1)}), bf16[2,64,256]{2,0,1:T(2,128)(2,1)S(1)}, u32[]{:S(2)}, u32[]{:S(2)}) %all-to-all-start.5) | async-done | bytes 65568 | tf_op jit(solution)/shard_map/all_to_all | solution.py:211
  149.2 5.8 %all-to-all-start.2 = ((bf16[2,64,256]{2,0,1:T(2,128)(2,1)}), bf16[2,64,256]{2,0,1:T(2,128)(2,1)S(1)}, u32[]{:S(2)}, u32[]{:S(2)}) async-start(bf16[2,64,256]{2,0,1:T(2,128)(2,1)} %copy.223), calls=%async_computation.2 | async-start | bytes 131072 | tf_op jit(solution)/shard_map/all_to_all | solution.py:204
  156.2 99.6 %psum.15 = f32[64,33]{0,1:T(8,128)S(1)} all-reduce(f32[64,33]{0,1:T(8,128)S(1)} %fusion.423), channel_id=1, replica_groups=mesh['ctx'=64,'tp'=8] {'ctx','tp'}, use_global_device_ids=true, to_apply=%region_1.2 | all-reduce | flops 2112 | bytes 16896 | tf_op jit(solution)/shard_map/psum | solution.py:229
  255.8 270.7 %psum.14 = f32[128,64]{0,1:T(8,128)S(1)} all-reduce(f32[128,64]{0,1:T(8,128)S(1)} %fusion.417), channel_id=1, replica_groups=mesh['ctx'=64,'tp'=8] {'ctx'}, use_global_device_ids=true, to_apply=%region_0.1 | all-reduce | flops 8192 | bytes 65536 | tf_op jit(solution)/shard_map/psum | solution.py:228
  528.0 8.4 %collective-permute-start.3 = (bf16[128,6]{1,0:T(8,128)(2,1)S(1)}, bf16[128,6]{1,0:T(8,128)(2,1)S(1)}, u32[]{:S(2)}, u32[]{:S(2)}) collective-permute-start(bf16[128,6]{1,0:T(8,128)(2,1)S(1)} %slice.333), channel_id=1, source_target_pairs={{8,0},{16,8},{24,16},{32,24},{40,32},{48,40},{56,48},{64,56},{72,6... | collective-permute-start | bytes 4616 | tf_op jit(solution)/shard_map/ppermute | solution.py:13
  537.3 1.0 fusion.51
  (140 shorter events, 42.9 us)
Async XLA Ops:
  0.6 8.8 %copy-start = (f32[128,64]{0,1:T(8,128)S(1)}, f32[128,64]{0,1:T(8,128)}, u32[]{:S(2)}) copy-start(f32[128,64]{0,1:T(8,128)} %param.16) | copy-start | bytes 98308
  1.5 32.3 %collective-permute-start = (bf16[128,6]{1,0:T(8,128)(2,1)S(1)}, bf16[128,6]{1,0:T(8,128)(2,1)S(1)}, u32[]{:S(2)}, u32[]{:S(2)}) collective-permute-start(bf16[128,6]{1,0:T(8,128)(2,1)S(1)} %slice.242), channel_id=1, source_target_pairs={{0,8},{8,16},{16,24},{24,32},{32,40},{40,48},{48,56},{56,64},{64,7... | collective-permute-start | bytes 4616 | tf_op jit(solution)/shard_map/ppermute | solution.py:13
  7.5 0.7 copy-start.9
  8.2 0.7 copy-start.5
  8.2 0.7 copy-start.7
  10.4 15.5 %copy-start.3 = (bf16[128,256]{1,0:T(8,128)(2,1)S(1)}, bf16[128,256]{1,0:T(8,128)(2,1)}, u32[]{:S(2)}) copy-start(bf16[128,256]{1,0:T(8,128)(2,1)} %param.12) | copy-start | bytes 196612
  10.4 27.7 %all-to-all-start = ((bf16[64,2,256]{2,1,0:T(2,128)(2,1)}), bf16[64,2,256]{2,1,0:T(2,128)(2,1)S(1)}, u32[]{:S(2)}, u32[]{:S(2)}) async-start(bf16[64,2,256]{2,1,0:T(2,128)(2,1)} %all_to_all.60), calls=%async_computation | async-start | bytes 131072 | tf_op jit(solution)/shard_map/all_to_all | solution.py:199
  25.9 3.6 copy-start.4
  26.0 59.8 %collective-permute-start.2 = (bf16[128,6]{1,0:T(8,128)(2,1)S(1)}, bf16[128,6]{1,0:T(8,128)(2,1)S(1)}, u32[]{:S(2)}, u32[]{:S(2)}) collective-permute-start(bf16[128,6]{1,0:T(8,128)(2,1)S(1)} %slice.274), channel_id=1, source_target_pairs={{0,8},{8,16},{16,24},{24,32},{32,40},{40,48},{48,56},{56,64},{64,7... | collective-permute-start | bytes 4616 | tf_op jit(solution)/shard_map/ppermute | solution.py:13
  29.6 2.7 copy-start.6
  29.6 56.3 %collective-permute-start.1 = (bf16[128,6]{1,0:T(8,128)(2,1)S(1)}, bf16[128,6]{1,0:T(8,128)(2,1)S(1)}, u32[]{:S(2)}, u32[]{:S(2)}) collective-permute-start(bf16[128,6]{1,0:T(8,128)(2,1)S(1)} %slice.258), channel_id=1, source_target_pairs={{0,8},{8,16},{16,24},{24,32},{32,40},{40,48},{48,56},{56,64},{64,7... | collective-permute-start | bytes 4616 | tf_op jit(solution)/shard_map/ppermute | solution.py:13
  33.0 0.9 copy-start.2
  33.1 0.7 copy-start.8
  33.8 0.8 copy-start.1
  38.1 21.5 %all-to-all-start.3 = ((bf16[64,2,256]{2,1,0:T(2,128)(2,1)}), bf16[64,2,256]{2,1,0:T(2,128)(2,1)S(1)}, u32[]{:S(2)}, u32[]{:S(2)}) async-start(bf16[64,2,256]{2,1,0:T(2,128)(2,1)} %all_to_all.67), calls=%async_computation.3 | async-start | bytes 131072 | tf_op jit(solution)/shard_map/all_to_all | solution.py:205
  80.9 17.0 %all-to-all-start.4 = ((bf16[2,64,256]{2,0,1:T(2,128)(2,1)}), bf16[2,64,256]{2,0,1:T(2,128)(2,1)S(1)}, u32[]{:S(2)}, u32[]{:S(2)}) async-start(bf16[2,64,256]{2,0,1:T(2,128)(2,1)} %copy.236), calls=%async_computation.4 | async-start | bytes 131072 | tf_op jit(solution)/shard_map/all_to_all | solution.py:210
  98.5 11.8 %collective-permute-start.5 = (bf16[128,6]{1,0:T(8,128)(2,1)S(1)}, bf16[128,6]{1,0:T(8,128)(2,1)S(1)}, u32[]{:S(2)}, u32[]{:S(2)}) collective-permute-start(bf16[128,6]{1,0:T(8,128)(2,1)S(1)} %slice.349), channel_id=1, source_target_pairs={{8,0},{16,8},{24,16},{32,24},{40,32},{48,40},{56,48},{64,56},{72,6... | collective-permute-start | bytes 4616 | tf_op jit(solution)/shard_map/ppermute | solution.py:13
  101.9 18.2 %all-to-all-start.1 = ((bf16[64,2,256]{2,1,0:T(2,128)(2,1)}), bf16[64,2,256]{2,1,0:T(2,128)(2,1)S(1)}, u32[]{:S(2)}, u32[]{:S(2)}) async-start(bf16[64,2,256]{2,1,0:T(2,128)(2,1)} %all_to_all.63), calls=%async_computation.1 | async-start | bytes 131072 | tf_op jit(solution)/shard_map/all_to_all | solution.py:198
  108.0 5.5 %collective-permute-start.4 = (bf16[128,6]{1,0:T(8,128)(2,1)S(1)}, bf16[128,6]{1,0:T(8,128)(2,1)S(1)}, u32[]{:S(2)}, u32[]{:S(2)}) collective-permute-start(bf16[128,6]{1,0:T(8,128)(2,1)S(1)} %slice.341), channel_id=1, source_target_pairs={{8,0},{16,8},{24,16},{32,24},{40,32},{48,40},{56,48},{64,56},{72,6... | collective-permute-start | bytes 4616 | tf_op jit(solution)/shard_map/ppermute | solution.py:13
  130.0 19.1 %all-to-all-start.5 = ((bf16[2,64,256]{2,0,1:T(2,128)(2,1)}), bf16[2,64,256]{2,0,1:T(2,128)(2,1)S(1)}, u32[]{:S(2)}, u32[]{:S(2)}) async-start(bf16[2,64,256]{2,0,1:T(2,128)(2,1)} %copy.242), calls=%async_computation.5 | async-start | bytes 131072 | tf_op jit(solution)/shard_map/all_to_all | solution.py:211
  149.2 378.0 %all-to-all-start.2 = ((bf16[2,64,256]{2,0,1:T(2,128)(2,1)}), bf16[2,64,256]{2,0,1:T(2,128)(2,1)S(1)}, u32[]{:S(2)}, u32[]{:S(2)}) async-start(bf16[2,64,256]{2,0,1:T(2,128)(2,1)} %copy.223), calls=%async_computation.2 | async-start | bytes 131072 | tf_op jit(solution)/shard_map/all_to_all | solution.py:204
  528.0 9.3 %collective-permute-start.3 = (bf16[128,6]{1,0:T(8,128)(2,1)S(1)}, bf16[128,6]{1,0:T(8,128)(2,1)S(1)}, u32[]{:S(2)}, u32[]{:S(2)}) collective-permute-start(bf16[128,6]{1,0:T(8,128)(2,1)S(1)} %slice.333), channel_id=1, source_target_pairs={{8,0},{16,8},{24,16},{32,24},{40,32},{48,40},{56,48},{64,56},{72,6... | collective-permute-start | bytes 4616 | tf_op jit(solution)/shard_map/ppermute | solution.py:13
where the time goes:
time: 544 us; the launch traced here: 539 us
  blocking collectives  370 us (68%)
  starting transfers between devices  72.2 us (13%)
  matrix products  39.1 us (7%)
  waiting for transfers between devices  37.1 us (7%)
  other arithmetic  9.16 us (2%)
  local copies, waits for them, and re-layouts  8.96 us (2%)
    psum x1, blocking collectives, on_device(): grad_proj = lax.psum(part_proj, 'ctx') * proj_scale  271 us
    psum x1, blocking collectives, on_device(): grad_basis = lax.psum(part_basis, ('ctx', 'tp')) * basis_scale  99.6 us
    ppermute x6, starting transfers between devices, passed_along(): lax.ppermute(value, axis, [(source, source + steps) for source in range(l...  23.4 us
    all_to_all x1, starting transfers between devices, on_device(): lax.all_to_all(filter_tok, 'ctx', split_axis=0, concat_axis=1, tiled=True)  15.5 us
    dot_general x3, matrix products, restore(): jnp.einsum('kt,nks->nts', outer[0], turned_re, precision=PRECISE)  13.3 us
    all_to_all x1, waiting for transfers between devices, on_device(): lax.all_to_all(carried_grad_chan, 'ctx', split_axis=1, concat_axis=0, til...  12 us
  transfers between devices with their start and end apart: 12, of which 7 were waited for; matrix products, arithmetic and copies ran while one was open for 7% of the time, Pallas kernels for 0%

commit v1 on v0

--- a/solution.py
+++ b/solution.py
@@ -5,6 +5,12 @@
 from jax.sharding import PartitionSpec as P
 
 PRECISE = lax.Precision.HIGHEST
+
+
+def summed_here(value, mesh_axis):
+    shards = lax.all_gather(value, mesh_axis, axis=0, tiled=False)
+    acc = shards.sum(axis=0)
+    return acc
 
 
 def passed_along(value, axis, steps):
@@ -225,7 +231,7 @@
     part_basis = jnp.dot(
         grad_hidden, basis_rows.T, precision=PRECISE, preferred_element_type=jnp.float32
     )
-    grad_proj = lax.psum(part_proj, "ctx") * proj_scale
+    grad_proj = summed_here(part_proj, "ctx") * proj_scale
     grad_basis = lax.psum(part_basis, ("ctx", "tp")) * basis_scale
     carried_grad_wide = carried_grad.astype(jnp.float32)
     grad_key_feat = (carried_grad_wide * value_feat).astype(jnp.bfloat16)

time: 544 us -> 289 us (0.53)
  blocking collectives: 370 us -> 129 us
  starting transfers between devices: 72.2 us -> 54.7 us
  between operations: 1.74 us -> 15.1 us
  matrix products: 39.1 us -> 30.6 us
    psum x1 -> x0, blocking collectives: 271 us -> none  [on_device(): grad_proj = lax.psum(part_proj, 'ctx') * proj_scale]
    all_to_all x0 -> x2, blocking collectives: none -> 31.9 us  [the longest x1 15.9 us: on_device(): lax.all_to_all(filter_grad_chan, 'ctx', split_axis=1, concat_axis=0, tile...]
    all_to_all x2 -> x0, starting transfers between devices: 12.9 us -> none  [the longest x1 6.95 us: on_device(): lax.all_to_all(filter_grad_chan, 'ctx', split_axis=1, concat_axis=0, tile...]
    all_to_all x2 -> x0, waiting for transfers between devices: 12.5 us -> none  [the longest x1 6.9 us: on_device(): lax.all_to_all(filter_grad_chan, 'ctx', split_axis=1, concat_axis=0, tile...]
    all_to_all x1, waiting for transfers between devices: 0.01 us -> 11.1 us  [on_device(): lax.all_to_all(long_chan, 'ctx', split_axis=1, concat_axis=0, tiled=True)]
    dot_general x3, matrix products: 13.3 us -> 2.78 us  [restore(): jnp.einsum('kt,nks->nts', outer[0], turned_re, precision=PRECISE)]
    ppermute x6, starting transfers between devices: 23.4 us -> 16.9 us  [passed_along(): lax.ppermute(value, axis, [(source, source + steps) for source in range(l...]
  transfers between devices with their start and end apart: 12 -> 11, of which waited for: 7 -> 6; matrix products, arithmetic and copies ran while one was open for 7% -> 12% of each run, Pallas kernels for 0% -> 0%
where the time goes in v1:
time: 289 us; the launch traced here: 284 us
  blocking collectives  129 us (45%)
  starting transfers between devices  54.7 us (19%)
  waiting for transfers between devices  35.6 us (12%)
  matrix products  30.6 us (11%)
  between operations  15.1 us (5%)
  other arithmetic  9.97 us (3%)
  local copies, waits for them, and re-layouts  9.34 us (3%)
    psum x1, blocking collectives, on_device(): grad_basis = lax.psum(part_basis, ('ctx', 'tp')) * basis_scale  96.7 us
    ppermute x6, starting transfers between devices, passed_along(): lax.ppermute(value, axis, [(source, source + steps) for source in range(l...  16.9 us
    all_to_all x1, blocking collectives, on_device(): lax.all_to_all(filter_grad_chan, 'ctx', split_axis=1, concat_axis=0, tile...  15.9 us
    all_to_all x1, blocking collectives, on_device(): lax.all_to_all(carried, 'ctx', split_axis=0, concat_axis=1, tiled=True)  15.9 us
    all_to_all x1, starting transfers between devices, on_device(): lax.all_to_all(filter_tok, 'ctx', split_axis=0, concat_axis=1, tiled=True)  15.3 us
    all_to_all x1, waiting for transfers between devices, on_device(): lax.all_to_all(carried_grad_chan, 'ctx', split_axis=1, concat_axis=0, til...  11.9 us
    all_to_all x1, waiting for transfers between devices, on_device(): lax.all_to_all(long_chan, 'ctx', split_axis=1, concat_axis=0, tiled=True)  11.1 us
    all_to_all x1, starting transfers between devices, on_device(): lax.all_to_all(grad_long, 'ctx', split_axis=0, concat_axis=1, tiled=True)  10.4 us
  transfers between devices with their start and end apart: 11, of which 6 were waited for; matrix products, arithmetic and copies ran while one was open for 12% of the time, Pallas kernels for 0%

profile of v1, /device:TPU:1, one launch (start us, length us, event | category | flops | bytes accessed | tf_op | source)
XLA Modules:
  0.0 283.8 jit_solution(11574025529743215977)
XLA Ops:
  8.1 4.6 %collective-permute-start = (bf16[128,6]{1,0:T(8,128)(2,1)S(1)}, bf16[128,6]{1,0:T(8,128)(2,1)S(1)}, u32[]{:S(2)}, u32[]{:S(2)}) collective-permute-start(bf16[128,6]{1,0:T(8,128)(2,1)S(1)} %slice.242), channel_id=1, source_target_pairs={{0,8},{8,16},{16,24},{24,32},{32,40},{40,48},{48,56},{56,64},{64,7... | collective-permute-start | bytes 4616 | tf_op jit(solution)/shard_map/ppermute | solution.py:19
  14.9 1.2 fusion.422
  17.8 15.3 %all-to-all-start = ((bf16[64,2,256]{2,1,0:T(2,128)(2,1)}), bf16[64,2,256]{2,1,0:T(2,128)(2,1)S(1)}, u32[]{:S(2)}, u32[]{:S(2)}) async-start(bf16[64,2,256]{2,1,0:T(2,128)(2,1)} %all_to_all.60), calls=%async_computation | async-start | bytes 131072 | tf_op jit(solution)/shard_map/all_to_all | solution.py:205
  34.0 3.5 %collective-permute-start.1 = (bf16[128,6]{1,0:T(8,128)(2,1)S(1)}, bf16[128,6]{1,0:T(8,128)(2,1)S(1)}, u32[]{:S(2)}, u32[]{:S(2)}) collective-permute-start(bf16[128,6]{1,0:T(8,128)(2,1)S(1)} %slice.258), channel_id=1, source_target_pairs={{0,8},{8,16},{16,24},{24,32},{32,40},{40,48},{48,56},{56,64},{64,7... | collective-permute-start | bytes 4616 | tf_op jit(solution)/shard_map/ppermute | solution.py:19
  38.4 2.0 collective-permute-start.2
  43.6 1.7 all-to-all-done
  45.3 10.4 %all-to-all-start.3 = ((bf16[64,2,256]{2,1,0:T(2,128)(2,1)}), bf16[64,2,256]{2,1,0:T(2,128)(2,1)S(1)}, u32[]{:S(2)}, u32[]{:S(2)}) async-start(bf16[64,2,256]{2,1,0:T(2,128)(2,1)} %all_to_all.67), calls=%async_computation.3 | async-start | bytes 131072 | tf_op jit(solution)/shard_map/all_to_all | solution.py:211
  59.7 7.8 %all-to-all-done.3 = bf16[64,2,256]{2,1,0:T(2,128)(2,1)S(1)} async-done(((bf16[64,2,256]{2,1,0:T(2,128)(2,1)}), bf16[64,2,256]{2,1,0:T(2,128)(2,1)S(1)}, u32[]{:S(2)}, u32[]{:S(2)}) %all-to-all-start.3) | async-done | bytes 65568 | tf_op jit(solution)/shard_map/all_to_all | solution.py:211
  75.5 1.0 fusion.19
  78.4 4.9 %all-to-all-start.4 = ((bf16[2,64,256]{2,0,1:T(2,128)(2,1)}), bf16[2,64,256]{2,0,1:T(2,128)(2,1)S(1)}, u32[]{:S(2)}, u32[]{:S(2)}) async-start(bf16[2,64,256]{2,0,1:T(2,128)(2,1)} %copy.236), calls=%async_computation.4 | async-start | bytes 131072 | tf_op jit(solution)/shard_map/all_to_all | solution.py:216
  83.6 11.9 %all-to-all-done.4 = bf16[2,64,256]{2,0,1:T(2,128)(2,1)S(1)} async-done(((bf16[2,64,256]{2,0,1:T(2,128)(2,1)}), bf16[2,64,256]{2,0,1:T(2,128)(2,1)S(1)}, u32[]{:S(2)}, u32[]{:S(2)}) %all-to-all-start.4) | async-done | bytes 65568 | tf_op jit(solution)/shard_map/all_to_all | solution.py:216
  96.5 15.9 %all_to_all.78 = bf16[64,2,256]{2,1,0:T(2,128)(2,1)S(1)} all-to-all(bf16[64,2,256]{2,1,0:T(2,128)(2,1)S(1)} %all_to_all.63), channel_id=1, replica_groups=mesh['ctx'=64,'tp'=8] {'ctx'}, dimensions={0} | all-to-all | bytes 131072 | tf_op jit(solution)/shard_map/all_to_all | solution.py:204
  121.8 15.9 %all_to_all.79 = bf16[2,64,256]{2,0,1:T(2,128)(2,1)S(1)} all-to-all(bf16[2,64,256]{2,0,1:T(2,128)(2,1)S(1)} %copy.242), channel_id=1, replica_groups=mesh['ctx'=64,'tp'=8] {'ctx'}, dimensions={1} | all-to-all | bytes 131072 | tf_op jit(solution)/shard_map/all_to_all | solution.py:217
  138.9 2.3 collective-permute-start.4
  141.2 2.1 collective-permute-start.5
  144.1 2.3 collective-permute-done.5
  146.5 1.0 fusion.44
  152.7 7.0 %all-to-all-start.2 = ((bf16[2,64,256]{2,0,1:T(2,128)(2,1)}), bf16[2,64,256]{2,0,1:T(2,128)(2,1)S(1)}, u32[]{:S(2)}, u32[]{:S(2)}) async-start(bf16[2,64,256]{2,0,1:T(2,128)(2,1)} %copy.223), calls=%async_computation.2 | async-start | bytes 131072 | tf_op jit(solution)/shard_map/all_to_all | solution.py:210
  159.8 1.0 fusion.37
  160.8 11.1 %all-to-all-done.2 = bf16[2,64,256]{2,0,1:T(2,128)(2,1)S(1)} async-done(((bf16[2,64,256]{2,0,1:T(2,128)(2,1)}), bf16[2,64,256]{2,0,1:T(2,128)(2,1)S(1)}, u32[]{:S(2)}, u32[]{:S(2)}) %all-to-all-start.2) | async-done | bytes 65568 | tf_op jit(solution)/shard_map/all_to_all | solution.py:210
  172.7 2.3 collective-permute-start.3
  175.7 96.7 %psum.7 = f32[64,33]{0,1:T(8,128)S(1)} all-reduce(f32[64,33]{0,1:T(8,128)S(1)} %fusion.423), channel_id=1, replica_groups=mesh['ctx'=64,'tp'=8] {'ctx','tp'}, use_global_device_ids=true, to_apply=%region_1.2 | all-reduce | flops 2112 | bytes 16896 | tf_op jit(solution)/shard_map/psum | solution.py:235
  273.0 1.0 fusion.51
  274.0 2.0 copy.273
  (136 shorter events, 43.5 us)
Async XLA Ops:
  7.2 9.0 %copy-start = (f32[128,64]{0,1:T(8,128)S(1)}, f32[128,64]{0,1:T(8,128)}, u32[]{:S(2)}) copy-start(f32[128,64]{0,1:T(8,128)} %param.16) | copy-start | bytes 98308
  7.2 35.3 %copy-start.2 = (bf16[128,256]{1,0:T(8,128)(2,1)S(1)}, bf16[128,256]{1,0:T(8,128)(2,1)}, u32[]{:S(2)}) copy-start(bf16[128,256]{1,0:T(8,128)(2,1)} %param.10) | copy-start | bytes 196612
  7.2 35.2 %copy-start.5 = (f32[128]{0:T(128)S(1)}, f32[128]{0:T(128)}, u32[]{:S(2)}) copy-start(f32[128]{0:T(128)} %param.18) | copy-start | bytes 1540
  7.2 35.4 %copy-start.1 = (bf16[128,256]{1,0:T(8,128)(2,1)S(1)}, bf16[128,256]{1,0:T(8,128)(2,1)}, u32[]{:S(2)}) copy-start(bf16[128,256]{1,0:T(8,128)(2,1)} %param.19) | copy-start | bytes 196612
  8.1 34.4 %collective-permute-start = (bf16[128,6]{1,0:T(8,128)(2,1)S(1)}, bf16[128,6]{1,0:T(8,128)(2,1)S(1)}, u32[]{:S(2)}, u32[]{:S(2)}) collective-permute-start(bf16[128,6]{1,0:T(8,128)(2,1)S(1)} %slice.242), channel_id=1, source_target_pairs={{0,8},{8,16},{16,24},{24,32},{32,40},{40,48},{48,56},{56,64},{64,7... | collective-permute-start | bytes 4616 | tf_op jit(solution)/shard_map/ppermute | solution.py:19
  17.8 27.5 %all-to-all-start = ((bf16[64,2,256]{2,1,0:T(2,128)(2,1)}), bf16[64,2,256]{2,1,0:T(2,128)(2,1)S(1)}, u32[]{:S(2)}, u32[]{:S(2)}) async-start(bf16[64,2,256]{2,1,0:T(2,128)(2,1)} %all_to_all.60), calls=%async_computation | async-start | bytes 131072 | tf_op jit(solution)/shard_map/all_to_all | solution.py:205
  34.0 49.4 %collective-permute-start.1 = (bf16[128,6]{1,0:T(8,128)(2,1)S(1)}, bf16[128,6]{1,0:T(8,128)(2,1)S(1)}, u32[]{:S(2)}, u32[]{:S(2)}) collective-permute-start(bf16[128,6]{1,0:T(8,128)(2,1)S(1)} %slice.258), channel_id=1, source_target_pairs={{0,8},{8,16},{16,24},{24,32},{32,40},{40,48},{48,56},{56,64},{64,7... | collective-permute-start | bytes 4616 | tf_op jit(solution)/shard_map/ppermute | solution.py:19
  38.4 45.2 %collective-permute-start.2 = (bf16[128,6]{1,0:T(8,128)(2,1)S(1)}, bf16[128,6]{1,0:T(8,128)(2,1)S(1)}, u32[]{:S(2)}, u32[]{:S(2)}) collective-permute-start(bf16[128,6]{1,0:T(8,128)(2,1)S(1)} %slice.274), channel_id=1, source_target_pairs={{0,8},{8,16},{16,24},{24,32},{32,40},{40,48},{48,56},{56,64},{64,7... | collective-permute-start | bytes 4616 | tf_op jit(solution)/shard_map/ppermute | solution.py:19
  45.3 22.2 %all-to-all-start.3 = ((bf16[64,2,256]{2,1,0:T(2,128)(2,1)}), bf16[64,2,256]{2,1,0:T(2,128)(2,1)S(1)}, u32[]{:S(2)}, u32[]{:S(2)}) async-start(bf16[64,2,256]{2,1,0:T(2,128)(2,1)} %all_to_all.67), calls=%async_computation.3 | async-start | bytes 131072 | tf_op jit(solution)/shard_map/all_to_all | solution.py:211
  74.9 8.5 %copy-start.3 = (bf16[128,256]{1,0:T(8,128)(2,1)S(1)}, bf16[128,256]{1,0:T(8,128)(2,1)}, u32[]{:S(2)}) copy-start(bf16[128,256]{1,0:T(8,128)(2,1)} %param.11) | copy-start | bytes 196612
  74.9 8.6 %copy-start.4 = (bf16[128,256]{1,0:T(8,128)(2,1)S(1)}, bf16[128,256]{1,0:T(8,128)(2,1)}, u32[]{:S(2)}) copy-start(bf16[128,256]{1,0:T(8,128)(2,1)} %param.12) | copy-start | bytes 196612
  78.4 17.1 %all-to-all-start.4 = ((bf16[2,64,256]{2,0,1:T(2,128)(2,1)}), bf16[2,64,256]{2,0,1:T(2,128)(2,1)S(1)}, u32[]{:S(2)}, u32[]{:S(2)}) async-start(bf16[2,64,256]{2,0,1:T(2,128)(2,1)} %copy.236), calls=%async_computation.4 | async-start | bytes 131072 | tf_op jit(solution)/shard_map/all_to_all | solution.py:216
  83.3 190.7 %all-gather.3.cloned.1.call-start = ((), (), s32[]{:S(2)}) async-start(), calls=%async_computation.6 | async-start | bytes 2129920 | tf_op jit(solution)/shard_map/all_gather | solution.py:11
  118.5 19.4 %copy-start.6 = (f32[128]{0:T(128)S(1)}, f32[128]{0:T(128)}, u32[]{:S(2)}) copy-start(f32[128]{0:T(128)} %param.17) | copy-start | bytes 1540
  138.9 5.2 %collective-permute-start.4 = (bf16[128,6]{1,0:T(8,128)(2,1)S(1)}, bf16[128,6]{1,0:T(8,128)(2,1)S(1)}, u32[]{:S(2)}, u32[]{:S(2)}) collective-permute-start(bf16[128,6]{1,0:T(8,128)(2,1)S(1)} %slice.341), channel_id=1, source_target_pairs={{8,0},{16,8},{24,16},{32,24},{40,32},{48,40},{56,48},{64,56},{72,6... | collective-permute-start | bytes 4616 | tf_op jit(solution)/shard_map/ppermute | solution.py:19
  141.2 5.2 %collective-permute-start.5 = (bf16[128,6]{1,0:T(8,128)(2,1)S(1)}, bf16[128,6]{1,0:T(8,128)(2,1)S(1)}, u32[]{:S(2)}, u32[]{:S(2)}) collective-permute-start(bf16[128,6]{1,0:T(8,128)(2,1)S(1)} %slice.349), channel_id=1, source_target_pairs={{8,0},{16,8},{24,16},{32,24},{40,32},{48,40},{56,48},{64,56},{72,6... | collective-permute-start | bytes 4616 | tf_op jit(solution)/shard_map/ppermute | solution.py:19
  152.7 19.2 %all-to-all-start.2 = ((bf16[2,64,256]{2,0,1:T(2,128)(2,1)}), bf16[2,64,256]{2,0,1:T(2,128)(2,1)S(1)}, u32[]{:S(2)}, u32[]{:S(2)}) async-start(bf16[2,64,256]{2,0,1:T(2,128)(2,1)} %copy.223), calls=%async_computation.2 | async-start | bytes 131072 | tf_op jit(solution)/shard_map/all_to_all | solution.py:210
  172.7 100.2 %collective-permute-start.3 = (bf16[128,6]{1,0:T(8,128)(2,1)S(1)}, bf16[128,6]{1,0:T(8,128)(2,1)S(1)}, u32[]{:S(2)}, u32[]{:S(2)}) collective-permute-start(bf16[128,6]{1,0:T(8,128)(2,1)S(1)} %slice.333), channel_id=1, source_target_pairs={{8,0},{16,8},{24,16},{32,24},{40,32},{48,40},{56,48},{64,56},{72,6... | collective-permute-start | bytes 4616 | tf_op jit(solution)/shard_map/ppermute | solution.py:19
Sparse Core Ops, SparseCore 0:
  139.0 75.6 all-gather.2
